TPU v7x, 512 devices: a whole 4x8x8 slice. The times are simulated.
512 devices in a mesh: ctx: 64 (over z, x, core), head: 8 (over y).
Axes of the slice: x: 4, y: 8, z: 8, core: 2. Of those that a mesh axis runs over, the one named last changes fastest.
Arguments:
- queries: bfloat16 [16384, 4096], P(('ctx', 'head')), may hold values from -6 to 6
- key_rows: bfloat16 [16384, 4096], P(('ctx', 'head')), may hold values from -6 to 6
- value_rows: bfloat16 [16384, 4096], P(('ctx', 'head')), may hold values from -6 to 6
- grad_out: bfloat16 [16384, 4096], P(('ctx', 'head')), may hold values from -6 to 6
Outputs:
- grad_query: bfloat16 [16384, 4096], P(('ctx', 'head'))
- grad_key: bfloat16 [16384, 4096], P(('ctx', 'head'))
- grad_value: bfloat16 [16384, 4096], P(('ctx', 'head'))
All inputs are finite; a program needn't handle non-finite values.
Results may differ from a plain program's by a relative error of at most 0.0021.
Values may be sent and summed in bfloat16 or wider, within the bound.
A program may use at most 128 MiB of HBM per device.

v0:
```python
import jax
import jax.numpy as jnp
from jax import lax
from jax.sharding import PartitionSpec as P

HEAD_DIM = 128
GROUP = 128


def exclusive_scans(forward_part, backward_part, axis):
    count = lax.axis_size(axis)
    fwd_total, fwd_excl = (forward_part, jnp.zeros_like(forward_part))
    bwd_total, bwd_excl = (backward_part, jnp.zeros_like(backward_part))
    shift = 1
    while shift < count:
        to_right = [(i, i + shift) for i in range(count - shift)]
        to_left = [(i + shift, i) for i in range(count - shift)]
        got_fwd = lax.ppermute(fwd_total, axis, to_right)
        got_bwd = lax.ppermute(bwd_total, axis, to_left)
        fwd_excl = fwd_excl + got_fwd
        bwd_excl = bwd_excl + got_bwd
        if shift * 2 < count:
            fwd_total = fwd_total + got_fwd
            bwd_total = bwd_total + got_bwd
        shift *= 2
    return (fwd_excl, bwd_excl)


def per_device(queries, key_rows, value_rows, grad_out):
    stacked = jnp.stack([queries, key_rows, value_rows, grad_out])
    q_all, k_all, v_all, d_all = lax.all_to_all(
        stacked, "head", split_axis=2, concat_axis=1, tiled=True
    )
    rows_here = q_all.shape[0]
    heads_here = q_all.shape[1] // HEAD_DIM
    scale = (HEAD_DIM * rows_here * lax.axis_size("ctx")) ** (-0.5)
    highest = lax.Precision.HIGHEST
    block = GROUP
    nblocks = rows_here // block
    shape_four = (nblocks, block, heads_here, HEAD_DIM)
    q_four = q_all.reshape(shape_four)
    k_four = k_all.reshape(shape_four)
    v_four = v_all.reshape(shape_four)
    d_four = d_all.reshape(shape_four)
    kv_blocks = jnp.einsum("ntha,nthb->nhab", v_four, k_four, preferred_element_type=jnp.float32)
    g_blocks = jnp.einsum("ntha,nthb->nhab", d_four, q_four, preferred_element_type=jnp.float32)
    kv_local = jnp.sum(kv_blocks, axis=0)
    g_local = jnp.sum(g_blocks, axis=0)
    kv_before, g_after = exclusive_scans(kv_local, g_local, "ctx")
    row_ids = lax.broadcasted_iota(jnp.int32, (nblocks, nblocks), 0)
    col_ids = lax.broadcasted_iota(jnp.int32, (nblocks, nblocks), 1)
    strict_lower = (col_ids < row_ids).astype(jnp.float32)
    strict_upper = (col_ids > row_ids).astype(jnp.float32)
    kv_in = kv_before[None] + jnp.einsum(
        "mn,nhab->mhab", strict_lower, kv_blocks, precision=highest
    )
    g_in = g_after[None] + jnp.einsum("mn,nhab->mhab", strict_upper, g_blocks, precision=highest)
    later = lax.broadcasted_iota(jnp.int32, (block, block), 0)
    earlier = lax.broadcasted_iota(jnp.int32, (block, block), 1)
    causal = (later >= earlier).astype(jnp.float32)
    scores = (
        jnp.einsum("nthd,nshd->nhts", q_four, k_four, preferred_element_type=jnp.float32)
        * (scale * causal)
    ).astype(jnp.bfloat16)
    dscores = (
        jnp.einsum("nthd,nshd->nhts", d_four, v_four, preferred_element_type=jnp.float32) * causal
    ).astype(jnp.bfloat16)
    k_float = k_four.astype(jnp.float32)
    v_float = v_four.astype(jnp.float32)
    d_float = d_four.astype(jnp.float32)
    grad_q = scale * (
        jnp.einsum("nhts,nshd->nthd", dscores, k_four, preferred_element_type=jnp.float32)
        + jnp.einsum("ntha,nhab->nthb", d_float, kv_in, precision=highest)
    )
    grad_k = scale * (
        jnp.einsum("nhts,nthd->nshd", dscores, q_four, preferred_element_type=jnp.float32)
        + jnp.einsum("ntha,nhab->nthb", v_float, g_in, precision=highest)
    )
    grad_v = jnp.einsum(
        "nhts,nthd->nshd", scores, d_four, preferred_element_type=jnp.float32
    ) + scale * jnp.einsum("nthb,nhab->ntha", k_float, g_in, precision=highest)
    flat_shape = (rows_here, heads_here * HEAD_DIM)
    grad_q = grad_q.reshape(flat_shape).astype(jnp.bfloat16)
    grad_k = grad_k.reshape(flat_shape).astype(jnp.bfloat16)
    grad_v = grad_v.reshape(flat_shape).astype(jnp.bfloat16)
    grads = jnp.stack([grad_q, grad_k, grad_v])
    result_q, result_k, result_v = lax.all_to_all(
        grads, "head", split_axis=1, concat_axis=2, tiled=True
    )
    return (result_q, result_k, result_v)


def solution(mesh):
    placed = (
        P(("ctx", "head"), None),
        P(("ctx", "head"), None),
        P(("ctx", "head"), None),
        P(("ctx", "head"), None),
    )
    return jax.shard_map(
        per_device,
        mesh=mesh,
        in_specs=placed,
        out_specs=(P(("ctx", "head"), None), P(("ctx", "head"), None), P(("ctx", "head"), None)),
        check_vma=False,
    )
```

profile of v0, /device:TPU:6, one launch (start us, length us, event | category | flops | bytes accessed | tf_op | source)
XLA Modules:
  0.0 192.5 jit_solution(13614894121044651994)
XLA Ops:
  0.6 1.3 pad_maximum_fusion
  2.0 4.7 %copy.93 = bf16[4,32,4096]{1,0,2:T(4,128)(2,1)} copy(bf16[4,32,4096]{2,1,0:T(8,128)(2,1)S(1)} %pad_maximum_fusion) | data formatting | bytes 2097152 | tf_op jit(solution)/shard_map/stack | solution.py:30
  6.6 7.0 %reshape.73 = bf16[8,2,32768]{2,1,0:T(2,128)(2,1)S(1)} reshape(bf16[4096,4,32]{2,1,0:T(4,128)(2,1)} %bitcast.57) | data formatting | bytes 2097152
  13.6 35.6 %all_to_all.30 = bf16[8,2,32768]{2,1,0:T(2,128)(2,1)S(1)} all-to-all(bf16[8,2,32768]{2,1,0:T(2,128)(2,1)S(1)} %reshape.73), channel_id=1, replica_groups=mesh['ctx'=64,'head'=8] {'head'}, dimensions={0} | all-to-all | bytes 2097152 | tf_op jit(solution)/shard_map/all_to_all | solution.py:31
  49.2 4.5 %reshape.74 = bf16[4096,4,32]{2,1,0:T(4,128)(2,1)} reshape(bf16[8,2,32768]{2,1,0:T(2,128)(2,1)S(1)} %all_to_all.30) | data formatting | bytes 2097152
  53.7 5.5 %copy.94 = bf16[4,32,8,512]{3,1,2,0:T(8,128)(2,1)S(1)} copy(bf16[4,32,8,512]{1,0,3,2:T(4,128)(2,1)} %bitcast.58) | data formatting | bytes 2097152 | tf_op jit(solution)/shard_map/all_to_all | solution.py:31
  59.5 0.3 fusion.55
  59.8 1.9 collective-permute-start
  62.0 0.2 fusion.54
  62.3 3.6 %collective-permute-start.6 = (f32[4,128,128]{2,1,0:T(8,128)S(1)}, f32[4,128,128]{2,1,0:T(8,128)S(1)}, u32[]{:S(2)}, u32[]{:S(2)}) collective-permute-start(f32[4,128,128]{2,1,0:T(8,128)S(1)} %get-tuple-element.10), channel_id=1, source_target_pairs={{8,0},{16,8},{24,16},{32,24},{40,32},{48,40},{56,48},{64,56},{72,6... | collective-permute-start | bytes 786440 | tf_op jit(solution)/shard_map/ppermute | solution.py:19
  65.9 1.5 collective-permute-done
  67.5 6.3 %collective-permute-start.1 = (f32[4,128,128]{2,1,0:T(8,128)S(1)}, f32[4,128,128]{2,1,0:T(8,128)S(1)}, u32[]{:S(2)}, u32[]{:S(2)}) collective-permute-start(f32[4,128,128]{2,1,0:T(8,128)S(1)} %add.88), channel_id=1, source_target_pairs={{0,16},{8,24},{16,32},{24,40},{32,48},{40,56},{48,64},{56,72},{64,... | collective-permute-start | bytes 786440 | tf_op jit(solution)/shard_map/ppermute | solution.py:18
  73.9 1.9 collective-permute-start.7
  75.8 1.9 collective-permute-done.1
  77.7 4.2 %collective-permute-start.2 = (f32[4,128,128]{2,1,0:T(8,128)S(1)}, f32[4,128,128]{2,1,0:T(8,128)S(1)}, u32[]{:S(2)}, u32[]{:S(2)}) collective-permute-start(f32[4,128,128]{2,1,0:T(8,128)S(1)} %add.90), channel_id=1, source_target_pairs={{0,32},{8,40},{16,48},{24,56},{32,64},{40,72},{48,80},{56,88},{64,... | collective-permute-start | bytes 786440 | tf_op jit(solution)/shard_map/ppermute | solution.py:18
  81.9 8.9 %collective-permute-done.7 = f32[4,128,128]{2,1,0:T(8,128)S(1)} collective-permute-done((f32[4,128,128]{2,1,0:T(8,128)S(1)}, f32[4,128,128]{2,1,0:T(8,128)S(1)}, u32[]{:S(2)}, u32[]{:S(2)}) %collective-permute-start.7) | collective-permute-done | bytes 262176 | tf_op jit(solution)/shard_map/ppermute | solution.py:19
  90.9 1.9 collective-permute-start.8
  92.8 4.3 %collective-permute-start.3 = (f32[4,128,128]{2,1,0:T(8,128)S(1)}, f32[4,128,128]{2,1,0:T(8,128)S(1)}, u32[]{:S(2)}, u32[]{:S(2)}) collective-permute-start(f32[4,128,128]{2,1,0:T(8,128)S(1)} %add.92), channel_id=1, source_target_pairs={{0,64},{8,72},{16,80},{24,88},{32,96},{40,104},{48,112},{56,120},{... | collective-permute-start | bytes 786440 | tf_op jit(solution)/shard_map/ppermute | solution.py:18
  97.2 5.4 %collective-permute-done.8 = f32[4,128,128]{2,1,0:T(8,128)S(1)} collective-permute-done((f32[4,128,128]{2,1,0:T(8,128)S(1)}, f32[4,128,128]{2,1,0:T(8,128)S(1)}, u32[]{:S(2)}, u32[]{:S(2)}) %collective-permute-start.8) | collective-permute-done | bytes 262176 | tf_op jit(solution)/shard_map/ppermute | solution.py:19
  102.6 1.3 collective-permute-start.9
  103.9 7.7 %collective-permute-start.4 = (f32[4,128,128]{2,1,0:T(8,128)S(1)}, f32[4,128,128]{2,1,0:T(8,128)S(1)}, u32[]{:S(2)}, u32[]{:S(2)}) collective-permute-start(f32[4,128,128]{2,1,0:T(8,128)S(1)} %add.94), channel_id=1, source_target_pairs={{0,128},{8,136},{16,144},{24,152},{32,160},{40,168},{48,176},{56,1... | collective-permute-start | bytes 786440 | tf_op jit(solution)/shard_map/ppermute | solution.py:18
  111.7 0.3 fusion.4
  112.0 1.3 collective-permute-start.10
  113.3 2.3 %collective-permute-done.4 = f32[4,128,128]{2,1,0:T(8,128)S(1)} collective-permute-done((f32[4,128,128]{2,1,0:T(8,128)S(1)}, f32[4,128,128]{2,1,0:T(8,128)S(1)}, u32[]{:S(2)}, u32[]{:S(2)}) %collective-permute-start.4) | collective-permute-done | bytes 262176 | tf_op jit(solution)/shard_map/ppermute | solution.py:18
  115.7 19.5 %collective-permute-start.5 = (f32[4,128,128]{2,1,0:T(8,128)S(1)}, f32[4,128,128]{2,1,0:T(8,128)S(1)}, u32[]{:S(2)}, u32[]{:S(2)}) collective-permute-start(f32[4,128,128]{2,1,0:T(8,128)S(1)} %add.96), channel_id=1, source_target_pairs={{0,256},{8,264},{16,272},{24,280},{32,288},{40,296},{48,304},{56,3... | collective-permute-start | bytes 786440 | tf_op jit(solution)/shard_map/ppermute | solution.py:18
  135.3 0.3 fusion.28
  135.6 0.3 fusion.18
  135.9 0.7 copy-done.2
  136.6 0.7 add.109
  137.3 1.3 collective-permute-start.11
  138.6 2.4 %collective-permute-done.5 = f32[4,128,128]{2,1,0:T(8,128)S(1)} collective-permute-done((f32[4,128,128]{2,1,0:T(8,128)S(1)}, f32[4,128,128]{2,1,0:T(8,128)S(1)}, u32[]{:S(2)}, u32[]{:S(2)}) %collective-permute-start.5) | collective-permute-done | bytes 262176 | tf_op jit(solution)/shard_map/ppermute | solution.py:18
  141.1 1.4 broadcast_add_fusion.1
  142.5 0.6 fusion.9
  143.1 0.2 copy.103
  143.3 0.8 convert_element_type.70
  144.1 9.8 %collective-permute-done.11 = f32[4,128,128]{2,1,0:T(8,128)} collective-permute-done((f32[4,128,128]{2,1,0:T(8,128)}, f32[4,128,128]{2,1,0:T(8,128)}, u32[]{:S(2)}, u32[]{:S(2)}) %collective-permute-start.11) | collective-permute-done | bytes 262176 | tf_op jit(solution)/shard_map/ppermute | solution.py:19
  153.9 1.3 add_add_fusion
  155.2 1.4 broadcast_add_fusion
  156.6 0.7 convolution_multiply_fusion.2
  157.2 0.6 fusion.8
  157.8 0.2 copy.110
  158.2 0.5 fusion.7
  158.7 0.2 copy.116
  159.1 0.7 copy.117
  159.8 30.3 %all_to_all.31 = bf16[3,256,512]{2,0,1:T(4,128)(2,1)S(1)} all-to-all(bf16[3,256,512]{2,0,1:T(4,128)(2,1)S(1)} %copy.117), channel_id=1, replica_groups=mesh['ctx'=64,'head'=8] {'head'}, dimensions={1} | all-to-all | bytes 1572864 | tf_op jit(solution)/shard_map/all_to_all | solution.py:87
  190.4 0.7 copy.124
  191.1 0.7 copy.125
  191.8 0.7 copy.126
  (35 shorter events, 1.6 us)
Async XLA Ops:
  59.8 7.7 %collective-permute-start = (f32[4,128,128]{2,1,0:T(8,128)S(1)}, f32[4,128,128]{2,1,0:T(8,128)S(1)}, u32[]{:S(2)}, u32[]{:S(2)}) collective-permute-start(f32[4,128,128]{2,1,0:T(8,128)S(1)} %get-tuple-element.12), channel_id=1, source_target_pairs={{0,8},{8,16},{16,24},{24,32},{32,40},{40,48},{48,56},{56,64},{64,7... | collective-permute-start | bytes 786440 | tf_op jit(solution)/shard_map/ppermute | solution.py:18
  62.3 11.5 %collective-permute-start.6 = (f32[4,128,128]{2,1,0:T(8,128)S(1)}, f32[4,128,128]{2,1,0:T(8,128)S(1)}, u32[]{:S(2)}, u32[]{:S(2)}) collective-permute-start(f32[4,128,128]{2,1,0:T(8,128)S(1)} %get-tuple-element.10), channel_id=1, source_target_pairs={{8,0},{16,8},{24,16},{32,24},{40,32},{48,40},{56,48},{64,56},{72,6... | collective-permute-start | bytes 786440 | tf_op jit(solution)/shard_map/ppermute | solution.py:19
  67.5 10.2 %collective-permute-start.1 = (f32[4,128,128]{2,1,0:T(8,128)S(1)}, f32[4,128,128]{2,1,0:T(8,128)S(1)}, u32[]{:S(2)}, u32[]{:S(2)}) collective-permute-start(f32[4,128,128]{2,1,0:T(8,128)S(1)} %add.88), channel_id=1, source_target_pairs={{0,16},{8,24},{16,32},{24,40},{32,48},{40,56},{48,64},{56,72},{64,... | collective-permute-start | bytes 786440 | tf_op jit(solution)/shard_map/ppermute | solution.py:18
  73.9 17.0 %collective-permute-start.7 = (f32[4,128,128]{2,1,0:T(8,128)S(1)}, f32[4,128,128]{2,1,0:T(8,128)S(1)}, u32[]{:S(2)}, u32[]{:S(2)}) collective-permute-start(f32[4,128,128]{2,1,0:T(8,128)S(1)} %add.101), channel_id=1, source_target_pairs={{16,0},{24,8},{32,16},{40,24},{48,32},{56,40},{64,48},{72,56},{80,... | collective-permute-start | bytes 786440 | tf_op jit(solution)/shard_map/ppermute | solution.py:19
  77.7 15.1 %collective-permute-start.2 = (f32[4,128,128]{2,1,0:T(8,128)S(1)}, f32[4,128,128]{2,1,0:T(8,128)S(1)}, u32[]{:S(2)}, u32[]{:S(2)}) collective-permute-start(f32[4,128,128]{2,1,0:T(8,128)S(1)} %add.90), channel_id=1, source_target_pairs={{0,32},{8,40},{16,48},{24,56},{32,64},{40,72},{48,80},{56,88},{64,... | collective-permute-start | bytes 786440 | tf_op jit(solution)/shard_map/ppermute | solution.py:18
  90.9 11.7 %collective-permute-start.8 = (f32[4,128,128]{2,1,0:T(8,128)S(1)}, f32[4,128,128]{2,1,0:T(8,128)S(1)}, u32[]{:S(2)}, u32[]{:S(2)}) collective-permute-start(f32[4,128,128]{2,1,0:T(8,128)S(1)} %add.103), channel_id=1, source_target_pairs={{32,0},{40,8},{48,16},{56,24},{64,32},{72,40},{80,48},{88,56},{96,... | collective-permute-start | bytes 786440 | tf_op jit(solution)/shard_map/ppermute | solution.py:19
  92.8 11.0 %collective-permute-start.3 = (f32[4,128,128]{2,1,0:T(8,128)S(1)}, f32[4,128,128]{2,1,0:T(8,128)S(1)}, u32[]{:S(2)}, u32[]{:S(2)}) collective-permute-start(f32[4,128,128]{2,1,0:T(8,128)S(1)} %add.92), channel_id=1, source_target_pairs={{0,64},{8,72},{16,80},{24,88},{32,96},{40,104},{48,112},{56,120},{... | collective-permute-start | bytes 786440 | tf_op jit(solution)/shard_map/ppermute | solution.py:18
  102.5 9.1 %copy-start = (f32[4,128,128]{2,1,0:T(8,128)}, f32[4,128,128]{2,1,0:T(8,128)S(1)}, u32[]{:S(2)}) copy-start(f32[4,128,128]{2,1,0:T(8,128)S(1)} %collective-permute-done.8) | copy-start | bytes 786436
  102.6 9.4 %collective-permute-start.9 = (f32[4,128,128]{2,1,0:T(8,128)S(1)}, f32[4,128,128]{2,1,0:T(8,128)S(1)}, u32[]{:S(2)}, u32[]{:S(2)}) collective-permute-start(f32[4,128,128]{2,1,0:T(8,128)S(1)} %add.105), channel_id=1, source_target_pairs={{64,0},{72,8},{80,16},{88,24},{96,32},{104,40},{112,48},{120,56},{... | collective-permute-start | bytes 786440 | tf_op jit(solution)/shard_map/ppermute | solution.py:19
  103.9 11.8 %collective-permute-start.4 = (f32[4,128,128]{2,1,0:T(8,128)S(1)}, f32[4,128,128]{2,1,0:T(8,128)S(1)}, u32[]{:S(2)}, u32[]{:S(2)}) collective-permute-start(f32[4,128,128]{2,1,0:T(8,128)S(1)} %add.94), channel_id=1, source_target_pairs={{0,128},{8,136},{16,144},{24,152},{32,160},{40,168},{48,176},{56,1... | collective-permute-start | bytes 786440 | tf_op jit(solution)/shard_map/ppermute | solution.py:18
  112.0 23.9 %copy-start.1 = (f32[4,128,128]{2,1,0:T(8,128)}, f32[4,128,128]{2,1,0:T(8,128)S(1)}, u32[]{:S(2)}) copy-start(f32[4,128,128]{2,1,0:T(8,128)S(1)} %collective-permute-done.9) | copy-start | bytes 786436
  112.0 23.8 %collective-permute-start.10 = (f32[4,128,128]{2,1,0:T(8,128)S(1)}, f32[4,128,128]{2,1,0:T(8,128)S(1)}, u32[]{:S(2)}, u32[]{:S(2)}) collective-permute-start(f32[4,128,128]{2,1,0:T(8,128)S(1)} %add.107), channel_id=1, source_target_pairs={{128,0},{136,8},{144,16},{152,24},{160,32},{168,40},{176,48},{184,... | collective-permute-start | bytes 786440 | tf_op jit(solution)/shard_map/ppermute | solution.py:19
  115.7 25.3 %collective-permute-start.5 = (f32[4,128,128]{2,1,0:T(8,128)S(1)}, f32[4,128,128]{2,1,0:T(8,128)S(1)}, u32[]{:S(2)}, u32[]{:S(2)}) collective-permute-start(f32[4,128,128]{2,1,0:T(8,128)S(1)} %add.96), channel_id=1, source_target_pairs={{0,256},{8,264},{16,272},{24,280},{32,288},{40,296},{48,304},{56,3... | collective-permute-start | bytes 786440 | tf_op jit(solution)/shard_map/ppermute | solution.py:18
  135.9 0.7 copy-start.2
  137.3 16.6 %collective-permute-start.11 = (f32[4,128,128]{2,1,0:T(8,128)}, f32[4,128,128]{2,1,0:T(8,128)}, u32[]{:S(2)}, u32[]{:S(2)}) collective-permute-start(f32[4,128,128]{2,1,0:T(8,128)} %add.109), channel_id=1, source_target_pairs={{256,0},{264,8},{272,16},{280,24},{288,32},{296,40},{304,48},{312,... | collective-permute-start | bytes 786440 | tf_op jit(solution)/shard_map/ppermute | solution.py:19
  155.2 3.8 %copy-start.3 = (bf16[1,256,512]{2,1,0:T(8,128)(2,1)S(1)}, bf16[1,256,512]{2,1,0:T(8,128)(2,1)}, u32[]{:S(2)}) copy-start(bf16[1,256,512]{2,1,0:T(8,128)(2,1)} %convert_element_type.70) | copy-start | bytes 786436
where the time goes:
time: 193 us
  blocking collectives  66 us (34%)
  starting transfers between devices  55.3 us (29%)
  waiting for transfers between devices  32.2 us (17%)
  local copies, waits for them, and re-layouts  27.6 us (14%)
  matrix products  6.56 us (3%)
  other arithmetic  3.85 us (2%)
    ppermute x6, starting transfers between devices, exclusive_scans(): got_fwd = lax.ppermute(fwd_total, axis, to_right)  43.9 us
    all_to_all x1, blocking collectives, per_device(): lax.all_to_all(stacked, 'head', split_axis=2, concat_axis=1, tiled=True)  35.6 us
    all_to_all x1, blocking collectives, per_device(): lax.all_to_all(grads, 'head', split_axis=1, concat_axis=2, tiled=True)  30.3 us
    ppermute x6, waiting for transfers between devices, exclusive_scans(): got_bwd = lax.ppermute(bwd_total, axis, to_left)  24.1 us
    unnamed x13, local copies, waits for them, and re-layouts  14.3 us
    ppermute x6, starting transfers between devices, exclusive_scans(): got_bwd = lax.ppermute(bwd_total, axis, to_left)  11.3 us
    ppermute x6, waiting for transfers between devices, exclusive_scans(): got_fwd = lax.ppermute(fwd_total, axis, to_right)  8.12 us
    all_to_all x1, local copies, waits for them, and re-layouts, per_device(): lax.all_to_all(stacked, 'head', split_axis=2, concat_axis=1, tiled=True)  5.51 us
  transfers between devices with their start and end apart: 12, of which 7 were waited for; matrix products, arithmetic and copies ran while one was open for 3% of the time, Pallas kernels for 0%

commit v1 on v0

--- a/solution.py
+++ b/solution.py
@@ -5,6 +5,22 @@
 
 HEAD_DIM = 128
 GROUP = 128
+
+
+def pairwise_exchange(x, axis, split, join):
+    ways, here = (lax.axis_size(axis), lax.axis_index(axis))
+    width = x.shape[split] // ways
+    shape = list(x.shape)
+    shape[split] = width
+    height = shape[join]
+    shape[join] = height * ways
+    full = jnp.zeros(shape, x.dtype)
+    for mask in range(ways):
+        part = lax.dynamic_slice_in_dim(x, (here ^ mask) * width, width, axis=split)
+        if mask:
+            part = lax.ppermute(part, axis, [(d, d ^ mask) for d in range(ways)])
+        full = lax.dynamic_update_slice_in_dim(full, part, (here ^ mask) * height, axis=join)
+    return full
 
 
 def exclusive_scans(forward_part, backward_part, axis):
@@ -28,9 +44,7 @@
 
 def per_device(queries, key_rows, value_rows, grad_out):
     stacked = jnp.stack([queries, key_rows, value_rows, grad_out])
-    q_all, k_all, v_all, d_all = lax.all_to_all(
-        stacked, "head", split_axis=2, concat_axis=1, tiled=True
-    )
+    q_all, k_all, v_all, d_all = pairwise_exchange(stacked, "head", 2, 1)
     rows_here = q_all.shape[0]
     heads_here = q_all.shape[1] // HEAD_DIM
     scale = (HEAD_DIM * rows_here * lax.axis_size("ctx")) ** (-0.5)

time: 193 us -> 171 us (0.89)
  the two profiles are of different devices: /device:TPU:6 before, /device:TPU:66 now
where the time goes in v1:
time: 171 us; the launch traced here: 170 us
  starting transfers between devices  78.3 us (46%)
  waiting for transfers between devices  46.2 us (27%)
  blocking collectives  31 us (18%)
  matrix products  6.56 us (4%)
  local copies, waits for them, and re-layouts  4.81 us (3%)
  other arithmetic  1.97 us (1%)
    ppermute x6, starting transfers between devices, exclusive_scans(): got_fwd = lax.ppermute(fwd_total, axis, to_right)  35.6 us
    all_to_all x1, blocking collectives, per_device(): lax.all_to_all(grads, 'head', split_axis=1, concat_axis=2, tiled=True)  31 us
    ppermute x7, starting transfers between devices, pairwise_exchange(): part = lax.ppermute(part, axis, [(d, d ^ mask) for d in range(ways)])  27.4 us
    ppermute x6, waiting for transfers between devices, exclusive_scans(): got_bwd = lax.ppermute(bwd_total, axis, to_left)  21.8 us
    ppermute x6, starting transfers between devices, exclusive_scans(): got_bwd = lax.ppermute(bwd_total, axis, to_left)  15.2 us
    ppermute x7, waiting for transfers between devices, pairwise_exchange(): part = lax.ppermute(part, axis, [(d, d ^ mask) for d in range(ways)])  13.7 us
    ppermute x6, waiting for transfers between devices, exclusive_scans(): got_fwd = lax.ppermute(fwd_total, axis, to_right)  10.7 us
  transfers between devices with their start and end apart: 19, of which 13 were waited for; matrix products, arithmetic and copies ran while one was open for 2% of the time, Pallas kernels for 0%

profile of v1, /device:TPU:66, one launch (start us, length us, event | category | flops | bytes accessed | tf_op | source)
XLA Modules:
  0.0 170.1 jit_solution(14607141227536725315)
XLA Ops:
  0.7 1.3 pad_maximum_fusion
  2.2 3.5 %collective-permute-start = (bf16[4,32,512]{2,1,0:T(8,128)(2,1)S(1)}, bf16[4,32,512]{2,1,0:T(8,128)(2,1)S(1)}, u32[]{:S(2)}, u32[]{:S(2)}) collective-permute-start(bf16[4,32,512]{2,1,0:T(8,128)(2,1)S(1)} %get-tuple-element.13), channel_id=1, source_target_pairs={{0,1},{1,0},{2,3},{3,2},{4,5},{5,4},{6,7},{7,6},{8,9},{9,8},{10,11... | collective-permute-start | bytes 393224 | tf_op jit(solution)/shard_map/ppermute | solution.py:21
  5.7 4.5 %collective-permute-start.1 = (bf16[4,32,512]{2,1,0:T(8,128)(2,1)S(1)}, bf16[4,32,512]{2,1,0:T(8,128)(2,1)S(1)}, u32[]{:S(2)}, u32[]{:S(2)}) collective-permute-start(bf16[4,32,512]{2,1,0:T(8,128)(2,1)S(1)} %get-tuple-element.12), channel_id=1, source_target_pairs={{0,2},{1,3},{2,0},{3,1},{4,6},{5,7},{6,4},{7,5},{8,10},{9,11},{10,... | collective-permute-start | bytes 393224 | tf_op jit(solution)/shard_map/ppermute | solution.py:21
  10.2 2.1 %collective-permute-start.2 = (bf16[4,32,512]{2,1,0:T(8,128)(2,1)S(1)}, bf16[4,32,512]{2,1,0:T(8,128)(2,1)S(1)}, u32[]{:S(2)}, u32[]{:S(2)}) collective-permute-start(bf16[4,32,512]{2,1,0:T(8,128)(2,1)S(1)} %get-tuple-element.11), channel_id=1, source_target_pairs={{0,3},{1,2},{2,1},{3,0},{4,7},{5,6},{6,5},{7,4},{8,11},{9,10},{10,... | collective-permute-start | bytes 393224 | tf_op jit(solution)/shard_map/ppermute | solution.py:21
  12.4 7.7 %collective-permute-start.3 = (bf16[4,32,512]{2,1,0:T(8,128)(2,1)S(1)}, bf16[4,32,512]{2,1,0:T(8,128)(2,1)S(1)}, u32[]{:S(2)}, u32[]{:S(2)}) collective-permute-start(bf16[4,32,512]{2,1,0:T(8,128)(2,1)S(1)} %get-tuple-element.10), channel_id=1, source_target_pairs={{0,4},{1,5},{2,6},{3,7},{4,0},{5,1},{6,2},{7,3},{8,12},{9,13},{10,... | collective-permute-start | bytes 393224 | tf_op jit(solution)/shard_map/ppermute | solution.py:21
  20.1 1.9 %collective-permute-start.4 = (bf16[4,32,512]{2,1,0:T(8,128)(2,1)S(1)}, bf16[4,32,512]{2,1,0:T(8,128)(2,1)S(1)}, u32[]{:S(2)}, u32[]{:S(2)}) collective-permute-start(bf16[4,32,512]{2,1,0:T(8,128)(2,1)S(1)} %get-tuple-element.9), channel_id=1, source_target_pairs={{0,5},{1,4},{2,7},{3,6},{4,1},{5,0},{6,3},{7,2},{8,13},{9,12},{10,... | collective-permute-start | bytes 393224 | tf_op jit(solution)/shard_map/ppermute | solution.py:21
  22.1 5.5 %collective-permute-start.5 = (bf16[4,32,512]{2,1,0:T(8,128)(2,1)S(1)}, bf16[4,32,512]{2,1,0:T(8,128)(2,1)S(1)}, u32[]{:S(2)}, u32[]{:S(2)}) collective-permute-start(bf16[4,32,512]{2,1,0:T(8,128)(2,1)S(1)} %get-tuple-element.8), channel_id=1, source_target_pairs={{0,6},{1,7},{2,4},{3,5},{4,2},{5,3},{6,0},{7,1},{8,14},{9,15},{10,... | collective-permute-start | bytes 393224 | tf_op jit(solution)/shard_map/ppermute | solution.py:21
  27.6 2.2 %collective-permute-start.6 = (bf16[4,32,512]{2,1,0:T(8,128)(2,1)S(1)}, bf16[4,32,512]{2,1,0:T(8,128)(2,1)S(1)}, u32[]{:S(2)}, u32[]{:S(2)}) collective-permute-start(bf16[4,32,512]{2,1,0:T(8,128)(2,1)S(1)} %get-tuple-element.7), channel_id=1, source_target_pairs={{0,7},{1,6},{2,5},{3,4},{4,3},{5,2},{6,1},{7,0},{8,15},{9,14},{10,... | collective-permute-start | bytes 393224 | tf_op jit(solution)/shard_map/ppermute | solution.py:21
  29.9 5.6 %collective-permute-done.4 = bf16[4,32,512]{2,1,0:T(8,128)(2,1)S(1)} collective-permute-done((bf16[4,32,512]{2,1,0:T(8,128)(2,1)S(1)}, bf16[4,32,512]{2,1,0:T(8,128)(2,1)S(1)}, u32[]{:S(2)}, u32[]{:S(2)}) %collective-permute-start.4) | collective-permute-done | bytes 131104 | tf_op jit(solution)/shard_map/ppermute | solution.py:21
  35.5 2.9 %collective-permute-done.5 = bf16[4,32,512]{2,1,0:T(8,128)(2,1)S(1)} collective-permute-done((bf16[4,32,512]{2,1,0:T(8,128)(2,1)S(1)}, bf16[4,32,512]{2,1,0:T(8,128)(2,1)S(1)}, u32[]{:S(2)}, u32[]{:S(2)}) %collective-permute-start.5) | collective-permute-done | bytes 131104 | tf_op jit(solution)/shard_map/ppermute | solution.py:21
  38.3 5.2 %collective-permute-done.6 = bf16[4,32,512]{2,1,0:T(8,128)(2,1)S(1)} collective-permute-done((bf16[4,32,512]{2,1,0:T(8,128)(2,1)S(1)}, bf16[4,32,512]{2,1,0:T(8,128)(2,1)S(1)}, u32[]{:S(2)}, u32[]{:S(2)}) %collective-permute-start.6) | collective-permute-done | bytes 131104 | tf_op jit(solution)/shard_map/ppermute | solution.py:21
  44.2 1.9 %collective-permute-start.13 = (f32[4,128,128]{2,1,0:T(8,128)S(1)}, f32[4,128,128]{2,1,0:T(8,128)S(1)}, u32[]{:S(2)}, u32[]{:S(2)}) collective-permute-start(f32[4,128,128]{2,1,0:T(8,128)S(1)} %get-tuple-element.18), channel_id=1, source_target_pairs={{8,0},{16,8},{24,16},{32,24},{40,32},{48,40},{56,48},{64,56},{72,6... | collective-permute-start | bytes 786440 | tf_op jit(solution)/shard_map/ppermute | solution.py:35
  46.3 0.3 fusion.55
  46.6 2.4 %collective-permute-start.7 = (f32[4,128,128]{2,1,0:T(8,128)S(1)}, f32[4,128,128]{2,1,0:T(8,128)S(1)}, u32[]{:S(2)}, u32[]{:S(2)}) collective-permute-start(f32[4,128,128]{2,1,0:T(8,128)S(1)} %get-tuple-element.20), channel_id=1, source_target_pairs={{0,8},{8,16},{16,24},{24,32},{32,40},{40,48},{48,56},{56,64},{64,7... | collective-permute-start | bytes 786440 | tf_op jit(solution)/shard_map/ppermute | solution.py:34
  49.0 1.1 collective-permute-done.13
  50.1 3.8 %collective-permute-start.14 = (f32[4,128,128]{2,1,0:T(8,128)S(1)}, f32[4,128,128]{2,1,0:T(8,128)S(1)}, u32[]{:S(2)}, u32[]{:S(2)}) collective-permute-start(f32[4,128,128]{2,1,0:T(8,128)S(1)} %add.165), channel_id=1, source_target_pairs={{16,0},{24,8},{32,16},{40,24},{48,32},{56,40},{64,48},{72,56},{80,... | collective-permute-start | bytes 786440 | tf_op jit(solution)/shard_map/ppermute | solution.py:35
  53.9 0.5 collective-permute-done.7
  54.4 3.4 %collective-permute-start.8 = (f32[4,128,128]{2,1,0:T(8,128)S(1)}, f32[4,128,128]{2,1,0:T(8,128)S(1)}, u32[]{:S(2)}, u32[]{:S(2)}) collective-permute-start(f32[4,128,128]{2,1,0:T(8,128)S(1)} %add.152), channel_id=1, source_target_pairs={{0,16},{8,24},{16,32},{24,40},{32,48},{40,56},{48,64},{56,72},{64,... | collective-permute-start | bytes 786440 | tf_op jit(solution)/shard_map/ppermute | solution.py:34
  57.8 2.3 %collective-permute-done.14 = f32[4,128,128]{2,1,0:T(8,128)S(1)} collective-permute-done((f32[4,128,128]{2,1,0:T(8,128)S(1)}, f32[4,128,128]{2,1,0:T(8,128)S(1)}, u32[]{:S(2)}, u32[]{:S(2)}) %collective-permute-start.14) | collective-permute-done | bytes 262176 | tf_op jit(solution)/shard_map/ppermute | solution.py:35
  60.1 5.0 %collective-permute-start.15 = (f32[4,128,128]{2,1,0:T(8,128)S(1)}, f32[4,128,128]{2,1,0:T(8,128)S(1)}, u32[]{:S(2)}, u32[]{:S(2)}) collective-permute-start(f32[4,128,128]{2,1,0:T(8,128)S(1)} %add.167), channel_id=1, source_target_pairs={{32,0},{40,8},{48,16},{56,24},{64,32},{72,40},{80,48},{88,56},{96,... | collective-permute-start | bytes 786440 | tf_op jit(solution)/shard_map/ppermute | solution.py:35
  65.2 1.3 collective-permute-done.8
  66.5 5.8 %collective-permute-start.9 = (f32[4,128,128]{2,1,0:T(8,128)S(1)}, f32[4,128,128]{2,1,0:T(8,128)S(1)}, u32[]{:S(2)}, u32[]{:S(2)}) collective-permute-start(f32[4,128,128]{2,1,0:T(8,128)S(1)} %add.154), channel_id=1, source_target_pairs={{0,32},{8,40},{16,48},{24,56},{32,64},{40,72},{48,80},{56,88},{64,... | collective-permute-start | bytes 786440 | tf_op jit(solution)/shard_map/ppermute | solution.py:34
  72.3 0.2 collective-permute-done.15
  72.6 1.9 %collective-permute-start.16 = (f32[4,128,128]{2,1,0:T(8,128)S(1)}, f32[4,128,128]{2,1,0:T(8,128)S(1)}, u32[]{:S(2)}, u32[]{:S(2)}) collective-permute-start(f32[4,128,128]{2,1,0:T(8,128)S(1)} %add.169), channel_id=1, source_target_pairs={{64,0},{72,8},{80,16},{88,24},{96,32},{104,40},{112,48},{120,56},{... | collective-permute-start | bytes 786440 | tf_op jit(solution)/shard_map/ppermute | solution.py:35
  74.5 4.8 %collective-permute-done.9 = f32[4,128,128]{2,1,0:T(8,128)S(1)} collective-permute-done((f32[4,128,128]{2,1,0:T(8,128)S(1)}, f32[4,128,128]{2,1,0:T(8,128)S(1)}, u32[]{:S(2)}, u32[]{:S(2)}) %collective-permute-start.9) | collective-permute-done | bytes 262176 | tf_op jit(solution)/shard_map/ppermute | solution.py:34
  79.3 4.3 %collective-permute-start.10 = (f32[4,128,128]{2,1,0:T(8,128)S(1)}, f32[4,128,128]{2,1,0:T(8,128)S(1)}, u32[]{:S(2)}, u32[]{:S(2)}) collective-permute-start(f32[4,128,128]{2,1,0:T(8,128)S(1)} %add.156), channel_id=1, source_target_pairs={{0,64},{8,72},{16,80},{24,88},{32,96},{40,104},{48,112},{56,120},{... | collective-permute-start | bytes 786440 | tf_op jit(solution)/shard_map/ppermute | solution.py:34
  83.6 0.2 collective-permute-done.16
  83.9 1.3 collective-permute-start.17
  85.2 4.2 %collective-permute-done.10 = f32[4,128,128]{2,1,0:T(8,128)S(1)} collective-permute-done((f32[4,128,128]{2,1,0:T(8,128)S(1)}, f32[4,128,128]{2,1,0:T(8,128)S(1)}, u32[]{:S(2)}, u32[]{:S(2)}) %collective-permute-start.10) | collective-permute-done | bytes 262176 | tf_op jit(solution)/shard_map/ppermute | solution.py:34
  89.5 11.2 %collective-permute-start.11 = (f32[4,128,128]{2,1,0:T(8,128)S(1)}, f32[4,128,128]{2,1,0:T(8,128)S(1)}, u32[]{:S(2)}, u32[]{:S(2)}) collective-permute-start(f32[4,128,128]{2,1,0:T(8,128)S(1)} %add.158), channel_id=1, source_target_pairs={{0,128},{8,136},{16,144},{24,152},{32,160},{40,168},{48,176},{56,1... | collective-permute-start | bytes 786440 | tf_op jit(solution)/shard_map/ppermute | solution.py:34
  100.7 9.5 %collective-permute-done.17 = f32[4,128,128]{2,1,0:T(8,128)S(1)} collective-permute-done((f32[4,128,128]{2,1,0:T(8,128)S(1)}, f32[4,128,128]{2,1,0:T(8,128)S(1)}, u32[]{:S(2)}, u32[]{:S(2)}) %collective-permute-start.17) | collective-permute-done | bytes 262176 | tf_op jit(solution)/shard_map/ppermute | solution.py:35
  110.2 1.3 collective-permute-start.18
  111.6 0.3 fusion.4
  111.9 8.5 %collective-permute-start.12 = (f32[4,128,128]{2,1,0:T(8,128)S(1)}, f32[4,128,128]{2,1,0:T(8,128)S(1)}, u32[]{:S(2)}, u32[]{:S(2)}) collective-permute-start(f32[4,128,128]{2,1,0:T(8,128)S(1)} %add.160), channel_id=1, source_target_pairs={{0,256},{8,264},{16,272},{24,280},{32,288},{40,296},{48,304},{56,3... | collective-permute-start | bytes 786440 | tf_op jit(solution)/shard_map/ppermute | solution.py:34
  120.4 8.5 %collective-permute-done.18 = f32[4,128,128]{2,1,0:T(8,128)S(1)} collective-permute-done((f32[4,128,128]{2,1,0:T(8,128)S(1)}, f32[4,128,128]{2,1,0:T(8,128)S(1)}, u32[]{:S(2)}, u32[]{:S(2)}) %collective-permute-start.18) | collective-permute-done | bytes 262176 | tf_op jit(solution)/shard_map/ppermute | solution.py:35
  129.0 1.4 broadcast_add_fusion
  130.4 0.6 fusion.16
  131.0 0.7 convolution_multiply_fusion.2
  131.8 1.4 broadcast_add_fusion.1
  133.2 0.6 fusion.10
  133.8 0.3 fusion.9
  134.4 0.3 fusion.8
  135.0 0.5 fusion.7
  135.9 0.7 copy.81
  136.6 31.0 %all_to_all.15 = bf16[3,256,512]{2,0,1:T(4,128)(2,1)S(1)} all-to-all(bf16[3,256,512]{2,0,1:T(4,128)(2,1)S(1)} %copy.81), channel_id=1, replica_groups=mesh['ctx'=64,'head'=8] {'head'}, dimensions={1} | all-to-all | bytes 1572864 | tf_op jit(solution)/shard_map/all_to_all | solution.py:101
  167.9 0.7 copy.88
  168.6 0.7 copy.89
  169.3 0.7 copy.90
  (45 shorter events, 2.8 us)
Async XLA Ops:
  2.2 19.9 %collective-permute-start = (bf16[4,32,512]{2,1,0:T(8,128)(2,1)S(1)}, bf16[4,32,512]{2,1,0:T(8,128)(2,1)S(1)}, u32[]{:S(2)}, u32[]{:S(2)}) collective-permute-start(bf16[4,32,512]{2,1,0:T(8,128)(2,1)S(1)} %get-tuple-element.13), channel_id=1, source_target_pairs={{0,1},{1,0},{2,3},{3,2},{4,5},{5,4},{6,7},{7,6},{8,9},{9,8},{10,11... | collective-permute-start | bytes 393224 | tf_op jit(solution)/shard_map/ppermute | solution.py:21
  5.7 21.9 %collective-permute-start.1 = (bf16[4,32,512]{2,1,0:T(8,128)(2,1)S(1)}, bf16[4,32,512]{2,1,0:T(8,128)(2,1)S(1)}, u32[]{:S(2)}, u32[]{:S(2)}) collective-permute-start(bf16[4,32,512]{2,1,0:T(8,128)(2,1)S(1)} %get-tuple-element.12), channel_id=1, source_target_pairs={{0,2},{1,3},{2,0},{3,1},{4,6},{5,7},{6,4},{7,5},{8,10},{9,11},{10,... | collective-permute-start | bytes 393224 | tf_op jit(solution)/shard_map/ppermute | solution.py:21
  10.2 19.6 %collective-permute-start.2 = (bf16[4,32,512]{2,1,0:T(8,128)(2,1)S(1)}, bf16[4,32,512]{2,1,0:T(8,128)(2,1)S(1)}, u32[]{:S(2)}, u32[]{:S(2)}) collective-permute-start(bf16[4,32,512]{2,1,0:T(8,128)(2,1)S(1)} %get-tuple-element.11), channel_id=1, source_target_pairs={{0,3},{1,2},{2,1},{3,0},{4,7},{5,6},{6,5},{7,4},{8,11},{9,10},{10,... | collective-permute-start | bytes 393224 | tf_op jit(solution)/shard_map/ppermute | solution.py:21
  12.4 17.5 %collective-permute-start.3 = (bf16[4,32,512]{2,1,0:T(8,128)(2,1)S(1)}, bf16[4,32,512]{2,1,0:T(8,128)(2,1)S(1)}, u32[]{:S(2)}, u32[]{:S(2)}) collective-permute-start(bf16[4,32,512]{2,1,0:T(8,128)(2,1)S(1)} %get-tuple-element.10), channel_id=1, source_target_pairs={{0,4},{1,5},{2,6},{3,7},{4,0},{5,1},{6,2},{7,3},{8,12},{9,13},{10,... | collective-permute-start | bytes 393224 | tf_op jit(solution)/shard_map/ppermute | solution.py:21
  20.1 15.4 %collective-permute-start.4 = (bf16[4,32,512]{2,1,0:T(8,128)(2,1)S(1)}, bf16[4,32,512]{2,1,0:T(8,128)(2,1)S(1)}, u32[]{:S(2)}, u32[]{:S(2)}) collective-permute-start(bf16[4,32,512]{2,1,0:T(8,128)(2,1)S(1)} %get-tuple-element.9), channel_id=1, source_target_pairs={{0,5},{1,4},{2,7},{3,6},{4,1},{5,0},{6,3},{7,2},{8,13},{9,12},{10,... | collective-permute-start | bytes 393224 | tf_op jit(solution)/shard_map/ppermute | solution.py:21
  22.1 16.2 %collective-permute-start.5 = (bf16[4,32,512]{2,1,0:T(8,128)(2,1)S(1)}, bf16[4,32,512]{2,1,0:T(8,128)(2,1)S(1)}, u32[]{:S(2)}, u32[]{:S(2)}) collective-permute-start(bf16[4,32,512]{2,1,0:T(8,128)(2,1)S(1)} %get-tuple-element.8), channel_id=1, source_target_pairs={{0,6},{1,7},{2,4},{3,5},{4,2},{5,3},{6,0},{7,1},{8,14},{9,15},{10,... | collective-permute-start | bytes 393224 | tf_op jit(solution)/shard_map/ppermute | solution.py:21
  27.6 16.0 %collective-permute-start.6 = (bf16[4,32,512]{2,1,0:T(8,128)(2,1)S(1)}, bf16[4,32,512]{2,1,0:T(8,128)(2,1)S(1)}, u32[]{:S(2)}, u32[]{:S(2)}) collective-permute-start(bf16[4,32,512]{2,1,0:T(8,128)(2,1)S(1)} %get-tuple-element.7), channel_id=1, source_target_pairs={{0,7},{1,6},{2,5},{3,4},{4,3},{5,2},{6,1},{7,0},{8,15},{9,14},{10,... | collective-permute-start | bytes 393224 | tf_op jit(solution)/shard_map/ppermute | solution.py:21
  44.2 5.8 %collective-permute-start.13 = (f32[4,128,128]{2,1,0:T(8,128)S(1)}, f32[4,128,128]{2,1,0:T(8,128)S(1)}, u32[]{:S(2)}, u32[]{:S(2)}) collective-permute-start(f32[4,128,128]{2,1,0:T(8,128)S(1)} %get-tuple-element.18), channel_id=1, source_target_pairs={{8,0},{16,8},{24,16},{32,24},{40,32},{48,40},{56,48},{64,56},{72,6... | collective-permute-start | bytes 786440 | tf_op jit(solution)/shard_map/ppermute | solution.py:35
  46.6 7.7 %collective-permute-start.7 = (f32[4,128,128]{2,1,0:T(8,128)S(1)}, f32[4,128,128]{2,1,0:T(8,128)S(1)}, u32[]{:S(2)}, u32[]{:S(2)}) collective-permute-start(f32[4,128,128]{2,1,0:T(8,128)S(1)} %get-tuple-element.20), channel_id=1, source_target_pairs={{0,8},{8,16},{16,24},{24,32},{32,40},{40,48},{48,56},{56,64},{64,7... | collective-permute-start | bytes 786440 | tf_op jit(solution)/shard_map/ppermute | solution.py:34
  50.1 10.0 %collective-permute-start.14 = (f32[4,128,128]{2,1,0:T(8,128)S(1)}, f32[4,128,128]{2,1,0:T(8,128)S(1)}, u32[]{:S(2)}, u32[]{:S(2)}) collective-permute-start(f32[4,128,128]{2,1,0:T(8,128)S(1)} %add.165), channel_id=1, source_target_pairs={{16,0},{24,8},{32,16},{40,24},{48,32},{56,40},{64,48},{72,56},{80,... | collective-permute-start | bytes 786440 | tf_op jit(solution)/shard_map/ppermute | solution.py:35
  54.4 12.1 %collective-permute-start.8 = (f32[4,128,128]{2,1,0:T(8,128)S(1)}, f32[4,128,128]{2,1,0:T(8,128)S(1)}, u32[]{:S(2)}, u32[]{:S(2)}) collective-permute-start(f32[4,128,128]{2,1,0:T(8,128)S(1)} %add.152), channel_id=1, source_target_pairs={{0,16},{8,24},{16,32},{24,40},{32,48},{40,56},{48,64},{56,72},{64,... | collective-permute-start | bytes 786440 | tf_op jit(solution)/shard_map/ppermute | solution.py:34
  60.1 12.4 %collective-permute-start.15 = (f32[4,128,128]{2,1,0:T(8,128)S(1)}, f32[4,128,128]{2,1,0:T(8,128)S(1)}, u32[]{:S(2)}, u32[]{:S(2)}) collective-permute-start(f32[4,128,128]{2,1,0:T(8,128)S(1)} %add.167), channel_id=1, source_target_pairs={{32,0},{40,8},{48,16},{56,24},{64,32},{72,40},{80,48},{88,56},{96,... | collective-permute-start | bytes 786440 | tf_op jit(solution)/shard_map/ppermute | solution.py:35
  66.5 12.8 %collective-permute-start.9 = (f32[4,128,128]{2,1,0:T(8,128)S(1)}, f32[4,128,128]{2,1,0:T(8,128)S(1)}, u32[]{:S(2)}, u32[]{:S(2)}) collective-permute-start(f32[4,128,128]{2,1,0:T(8,128)S(1)} %add.154), channel_id=1, source_target_pairs={{0,32},{8,40},{16,48},{24,56},{32,64},{40,72},{48,80},{56,88},{64,... | collective-permute-start | bytes 786440 | tf_op jit(solution)/shard_map/ppermute | solution.py:34
  72.6 11.2 %collective-permute-start.16 = (f32[4,128,128]{2,1,0:T(8,128)S(1)}, f32[4,128,128]{2,1,0:T(8,128)S(1)}, u32[]{:S(2)}, u32[]{:S(2)}) collective-permute-start(f32[4,128,128]{2,1,0:T(8,128)S(1)} %add.169), channel_id=1, source_target_pairs={{64,0},{72,8},{80,16},{88,24},{96,32},{104,40},{112,48},{120,56},{... | collective-permute-start | bytes 786440 | tf_op jit(solution)/shard_map/ppermute | solution.py:35
  79.3 10.1 %collective-permute-start.10 = (f32[4,128,128]{2,1,0:T(8,128)S(1)}, f32[4,128,128]{2,1,0:T(8,128)S(1)}, u32[]{:S(2)}, u32[]{:S(2)}) collective-permute-start(f32[4,128,128]{2,1,0:T(8,128)S(1)} %add.156), channel_id=1, source_target_pairs={{0,64},{8,72},{16,80},{24,88},{32,96},{40,104},{48,112},{56,120},{... | collective-permute-start | bytes 786440 | tf_op jit(solution)/shard_map/ppermute | solution.py:34
  83.9 26.3 %collective-permute-start.17 = (f32[4,128,128]{2,1,0:T(8,128)S(1)}, f32[4,128,128]{2,1,0:T(8,128)S(1)}, u32[]{:S(2)}, u32[]{:S(2)}) collective-permute-start(f32[4,128,128]{2,1,0:T(8,128)S(1)} %add.171), channel_id=1, source_target_pairs={{128,0},{136,8},{144,16},{152,24},{160,32},{168,40},{176,48},{184,... | collective-permute-start | bytes 786440 | tf_op jit(solution)/shard_map/ppermute | solution.py:35
  89.5 22.4 %collective-permute-start.11 = (f32[4,128,128]{2,1,0:T(8,128)S(1)}, f32[4,128,128]{2,1,0:T(8,128)S(1)}, u32[]{:S(2)}, u32[]{:S(2)}) collective-permute-start(f32[4,128,128]{2,1,0:T(8,128)S(1)} %add.158), channel_id=1, source_target_pairs={{0,128},{8,136},{16,144},{24,152},{32,160},{40,168},{48,176},{56,1... | collective-permute-start | bytes 786440 | tf_op jit(solution)/shard_map/ppermute | solution.py:34
  110.2 18.7 %collective-permute-start.18 = (f32[4,128,128]{2,1,0:T(8,128)S(1)}, f32[4,128,128]{2,1,0:T(8,128)S(1)}, u32[]{:S(2)}, u32[]{:S(2)}) collective-permute-start(f32[4,128,128]{2,1,0:T(8,128)S(1)} %add.173), channel_id=1, source_target_pairs={{256,0},{264,8},{272,16},{280,24},{288,32},{296,40},{304,48},{312,... | collective-permute-start | bytes 786440 | tf_op jit(solution)/shard_map/ppermute | solution.py:35
  111.9 19.8 %collective-permute-start.12 = (f32[4,128,128]{2,1,0:T(8,128)S(1)}, f32[4,128,128]{2,1,0:T(8,128)S(1)}, u32[]{:S(2)}, u32[]{:S(2)}) collective-permute-start(f32[4,128,128]{2,1,0:T(8,128)S(1)} %add.160), channel_id=1, source_target_pairs={{0,256},{8,264},{16,272},{24,280},{32,288},{40,296},{48,304},{56,3... | collective-permute-start | bytes 786440 | tf_op jit(solution)/shard_map/ppermute | solution.py:34
